TPU v7x, 32 devices: a whole 2x2x4 slice. The times are simulated.
32 devices in a mesh: parts: 2 (over y), ctx: 4 (over z), mp: 4 (over x, core).
Axes of the slice: x: 2, y: 2, z: 4, core: 2. Of those that a mesh axis runs over, the one named last changes fastest.
Arguments:
- inputs: bfloat16 [1024, 3, 4096], P(('parts', 'ctx'), None, 'mp'), parts along dimension 0, may hold values from -6 to 6
- short_filter: bfloat16 [3, 3, 4096], P(None, None, 'mp'), may hold values from -3.5 to 3.5
- long_filter: bfloat16 [256, 128], P('mp'), may hold values from -0.5 to 0.5
- skip_gain: float32 [4096], P('mp'), may hold values from -1 to 1
- queries: bfloat16 [1024, 4096], P(('parts', 'ctx'), 'mp'), parts along dimension 0, may hold values from -6 to 6
- key_rows: bfloat16 [1024, 4096], P(('parts', 'ctx'), 'mp'), parts along dimension 0, may hold values from -6 to 6
- out_weight: bfloat16 [4096, 4096], P('mp'), may hold values from -0.25 to 0.25
Outputs:
- block_output: bfloat16 [1024, 4096], P(('parts', 'ctx'), 'mp'), parts along dimension 0
There are 2 independent parts, one for each index of `parts`. A program takes and returns all parts, laid end to end along the dimension named above; an argument that names none is the same for every part. Nothing has to cross between parts.
All inputs are finite; a program needn't handle non-finite values.
Results may differ from a plain program's by a relative error of at most 0.014.
Values may be sent and summed in bfloat16 or wider, within the bound.
A program may use at most 64 MiB of HBM per device.

v0:
```python
import jax
import jax.numpy as jnp
from jax import lax
from jax.sharding import PartitionSpec as P

HEAD_DIM = 128


masked_score = -1e30


def passed_along(value, axis, steps):
    count = lax.axis_size(axis)
    initial, last = (max(0, -steps), min(count, count - steps))
    return lax.ppermute(value, axis, [(source, source + steps) for source in range(initial, last)])


def toeplitz_taps(filters, row_count):
    group_count = filters.shape[0]
    tap_count = filters.shape[1]
    span = row_count + tap_count - 1
    flipped = filters[:, ::-1]
    padded_taps = jnp.concatenate(
        [flipped, jnp.zeros((group_count, row_count), filters.dtype)], axis=1
    )
    repeated = jnp.tile(padded_taps, (1, row_count))
    return repeated[:, : row_count * span].reshape(group_count, row_count, span)


def short_features(extended, short_filter, row_count):
    tap_count = short_filter.shape[0]
    features = jnp.zeros((row_count,) + extended.shape[1:], jnp.float32)
    for lag_index in range(tap_count):
        delayed = extended[
            tap_count - 1 - lag_index : tap_count - 1 - lag_index + row_count
        ].astype(jnp.float32)
        features = features + short_filter[lag_index].astype(jnp.float32)[None] * delayed
    return features


def attend(running, head_queries, query_pos, key_piece, value_piece):
    running_max, weight_sum, accumulated = running
    key_count = key_piece.shape[0]
    head_count = head_queries.shape[1]
    key_heads = key_piece.reshape(key_count, head_count, -1)
    value_heads = value_piece.reshape(key_count, head_count, -1)
    scores = jnp.einsum(
        "qhd,khd->hqk", head_queries, key_heads, preferred_element_type=jnp.float32
    ) * head_queries.shape[2] ** (-0.5)
    key_pos = lax.iota(jnp.int32, key_count)
    allowed = (key_pos[None, :] <= query_pos[:, None])[None]
    new_max = jnp.maximum(running_max, jnp.max(jnp.where(allowed, scores, masked_score), axis=2))
    probabilities = jnp.where(allowed, jnp.exp(scores - new_max[..., None]), 0.0)
    weight_sum = jnp.sum(probabilities, axis=2)
    mixed = jnp.einsum(
        "hqk,khd->hqd",
        probabilities.astype(jnp.bfloat16),
        value_heads,
        preferred_element_type=jnp.float32,
    )
    accumulated = mixed
    return (new_max, weight_sum, accumulated)


def start_state(head_count, row_count, width):
    return (
        jnp.full((head_count, row_count), masked_score, jnp.float32),
        jnp.zeros((head_count, row_count), jnp.float32),
        jnp.zeros((head_count, row_count, width), jnp.float32),
    )


def finish(running):
    running_max, weight_sum, accumulated = running
    result = accumulated / weight_sum[..., None]
    return jnp.transpose(result, (1, 0, 2)).reshape(result.shape[1], -1).astype(jnp.bfloat16)


def per_device(inputs, short_filter, long_filter, skip_gain, queries, key_rows, out_weight):
    row_count = inputs.shape[0]
    channels = inputs.shape[2]
    groups = long_filter.shape[0]
    tap_count = long_filter.shape[1]
    short_reach = short_filter.shape[0] - 1
    position = lax.axis_index("ctx")
    rim = passed_along(inputs[row_count - short_reach :], "ctx", 1)
    extended = jnp.concatenate([rim, inputs], axis=0)
    features = short_features(extended, short_filter, row_count)
    gate_product = (features[:, 1] * features[:, 2]).astype(jnp.bfloat16)
    gate_prev = passed_along(gate_product[row_count - (tap_count - 1) :], "ctx", 1)
    gate_ext = jnp.concatenate([gate_prev, gate_product], axis=0)
    toeplitz = toeplitz_taps(long_filter, row_count)
    filtered = jnp.einsum(
        "gtr,rgc->tgc",
        toeplitz,
        gate_ext.reshape(row_count + tap_count - 1, groups, channels // groups),
        preferred_element_type=jnp.float32,
    ).reshape(row_count, channels)
    values = (
        features[:, 0] * (filtered + skip_gain[None] * gate_product.astype(jnp.float32))
    ).astype(jnp.bfloat16)
    head_count = channels // HEAD_DIM
    head_queries = queries.reshape(row_count, head_count, HEAD_DIM)
    query_pos = position * row_count + lax.iota(jnp.int32, row_count)
    initial = start_state(head_count, row_count, HEAD_DIM)
    folded = attend(
        initial,
        head_queries,
        query_pos,
        lax.all_gather(key_rows, "ctx", axis=0, tiled=True),
        lax.all_gather(values, "ctx", axis=0, tiled=True),
    )
    attended = finish(folded)
    partial_out = jnp.dot(attended, out_weight, preferred_element_type=jnp.float32)
    return lax.psum_scatter(partial_out.astype(jnp.bfloat16), "mp", scatter_dimension=1, tiled=True)


def solution(mesh):
    placed = (
        P(("parts", "ctx"), None, "mp"),
        P(None, None, "mp"),
        P("mp", None),
        P("mp"),
        P(("parts", "ctx"), "mp"),
        P(("parts", "ctx"), "mp"),
        P("mp", None),
    )
    return jax.shard_map(
        per_device, mesh=mesh, in_specs=placed, out_specs=P(("parts", "ctx"), "mp"), check_vma=False
    )
```

profile of v0, /device:TPU:28, one launch (start us, length us, event | category | flops | bytes accessed | tf_op | source)
XLA Modules:
  0.0 111.8 jit_solution(9529709808530906281)
XLA Ops:
  6.5 0.9 slice.38
  7.4 1.3 %collective-permute-start = (bf16[2,3,1024]{2,0,1:T(2,128)(2,1)S(1)}, bf16[2,3,1024]{2,0,1:T(2,128)(2,1)S(1)}, u32[]{:S(2)}, u32[]{:S(2)}) collective-permute-start(bf16[2,3,1024]{2,0,1:T(2,128)(2,1)S(1)} %slice.38), channel_id=1, source_target_pairs={{0,4},{4,8},{8,12},{1,5},{5,9},{9,13},{2,6},{6,10},{10,14},{3,7},{... | collective-permute-start | bytes 36872 | tf_op jit(solution)/shard_map/ppermute | solution.py:15
  8.7 1.8 %copy.12 = bf16[128,1024]{0,1:T(8,128)(2,1)} copy(bf16[128,1024]{1,0:T(8,128)(2,1)} %param.12) | data formatting | bytes 524288 | tf_op args[5]
  10.5 0.0 all-gather.3.cloned.1.call-update
  10.5 0.0 all-gather.5.cloned.1.call-start
  10.6 0.7 bitcast_convert_fusion.2
  11.3 1.7 %collective-permute-done = bf16[2,3,1024]{2,0,1:T(2,128)(2,1)S(1)} collective-permute-done((bf16[2,3,1024]{2,0,1:T(2,128)(2,1)S(1)}, bf16[2,3,1024]{2,0,1:T(2,128)(2,1)S(1)}, u32[]{:S(2)}, u32[]{:S(2)}) %collective-permute-start) | collective-permute-done | bytes 12320 | tf_op jit(solution)/shard_map/ppermute | solution.py:15
  13.0 2.4 %multiply_add_fusion = f32[128,3,1024]{2,0,1:T(8,128)S(1)} fusion(bf16[128,3,1024]{2,0,1:T(8,128)(2,1)} %param.7, bf16[2,3,1024]{2,0,1:T(2,128)(2,1)S(1)} %collective-permute-done, f32[3,1024]{1,0:T(4,128)S(1)} %get-tuple-element.6, f32[3,1024]{1,0:T(4,128)S(1)} %get-tuple-element.7, f32[3,1024]{1,0:T(4,128)S(1)} %get-tuple-element.5), kind=kLoop, calls=%fused_computation.5 | loop fusion | flops 5505024 | bytes 2408448 | tf_op jit(solution)/shard_map/add | solution.py:37
  15.4 0.1 fusion.10
  15.4 0.1 slice_bitcast_fusion.1
  15.5 1.3 %collective-permute-start.1 = (bf16[127,1024]{1,0:T(8,128)(2,1)S(1)}, bf16[127,1024]{1,0:T(8,128)(2,1)S(1)}, u32[]{:S(2)}, u32[]{:S(2)}) collective-permute-start(bf16[127,1024]{1,0:T(8,128)(2,1)S(1)} %slice_bitcast_fusion.1), channel_id=1, source_target_pairs={{0,4},{4,8},{8,12},{1,5},{5,9},{9,13},{2,6},{6,10},{10,14},{3,7},{... | collective-permute-start | bytes 780296 | tf_op jit(solution)/shard_map/ppermute | solution.py:15
  16.8 0.1 rev.3
  16.9 0.3 tile.4
  17.2 2.6 %copy.20 = bf16[8,8,128,256]{3,1,2,0:T(8,128)(2,1)S(1)} copy(bf16[8,8,128,256]{3,2,1,0:T(8,128)(2,1)S(1)} %bitcast.51) | data formatting | bytes 8388608
  19.8 2.2 %slice.54 = bf16[64,32640]{1,0:T(8,128)(2,1)} slice(bf16[64,32768]{1,0:T(8,128)(2,1)S(1)} %bitcast.52), slice={[0:64], [0:32640]} | slice | bytes 8355840 | tf_op jit(solution)/shard_map/slice | solution.py:27
  22.1 15.8 %reshape.58 = bf16[64,128,255]{2,1,0:T(8,128)(2,1)} reshape(bf16[64,32640]{1,0:T(8,128)(2,1)} %slice.54) | data formatting | bytes 8355840 | tf_op jit(solution)/shard_map/reshape | solution.py:27
  37.9 0.1 fusion.25
  38.0 0.1 pad_maximum_fusion.1
  38.0 0.2 copy.15
  38.3 3.4 %fusion.18 = f32[64,16,128]{2,1,0:T(8,128)S(1)} fusion(bf16[255,64,16]{0,2,1:T(8,128)(2,1)S(1)} %bitcast.53, bf16[64,128,255]{2,1,0:T(8,128)(2,1)} %reshape.58), kind=kOutput, calls=%fused_computation.35 | convolution fusion | flops 66846720 | bytes 5224448 | tf_op jit(solution)/shard_map/gtr,rgc->tgc/dot_general | solution.py:93
  41.6 0.2 copy.16
  41.9 0.9 fusion.12
  42.8 0.0 reduce-scatter.2.cloned.1.call-start
  42.8 0.1 iota_compare_fusion
  43.0 0.0 all-gather.3.cloned.1.call-done
  43.0 1.8 %select_reduce_fusion = (f32[8,128]{1,0:T(8,128)S(1)}, f32[8,128,512]{2,1,0:T(8,128)S(1)}) fusion(pred[128,512]{1,0:T(8,128)(4,1)S(1)} %iota_compare_fusion, bf16[512,8,128]{0,2,1:T(8,128)(2,1)} %bitcast.56, bf16[128,1024]{1,0:T(8,128)(2,1)S(1)} %copy-done), kind=kOutput, calls=%fused_computation.2 | convolution fusion | flops 135789568 | bytes 3477504 | tf_op jit(solution)/shard_map/qhd,khd->hqk/dot_general | solution.py:47
  44.8 0.6 fusion
  45.4 26.2 %all-gather.5.cloned.1.call-done = bf16[512,1024]{1,0:T(8,128)(2,1)} async-done(((bf16[128,1024]{1,0:T(8,128)(2,1)}), bf16[512,1024]{1,0:T(8,128)(2,1)}) %all-gather.5.cloned.1.call-update) | async-done | bytes 1048592 | tf_op jit(solution)/shard_map/all_gather | solution.py:111
  71.6 1.5 %copy.17 = bf16[512,1024]{0,1:T(8,128)(2,1)S(1)} copy(bf16[512,1024]{1,0:T(8,128)(2,1)} %all-gather.5.cloned.1.call-done) | data formatting | bytes 2097152 | tf_op jit(solution)/shard_map/all_gather | solution.py:111
  73.1 0.6 fusion.3
  73.8 5.6 %convolution_convert_fusion = bf16[128,4096]{1,0:T(8,128)(2,1)} fusion(bf16[128,1024]{0,1:T(8,128)(2,1)S(1)} %bitcast.57, bf16[1024,4096]{1,0:T(8,128)(2,1)} %param.13), kind=kOutput, calls=%fused_computation | convolution fusion | flops 1074266112 | bytes 9699328 | tf_op jit(solution)/shard_map/dot_general | solution.py:114
  79.5 25.8 %reduce-scatter.2.cloned.1.call-done = bf16[128,1024]{1,0:T(8,128)(2,1)} async-done(((bf16[128,4096]{1,0:T(8,128)(2,1)}), bf16[128,1024]{1,0:T(8,128)(2,1)}) %reduce-scatter.2.cloned.1.call-update) | async-done | bytes 262160 | tf_op jit(solution)/shard_map/reduce_scatter | solution.py:115
  (13 shorter events, 0.1 us)
Async XLA Ops:
  6.5 36.5 %copy-start = (bf16[128,1024]{1,0:T(8,128)(2,1)S(1)}, bf16[128,1024]{1,0:T(8,128)(2,1)}, u32[]{:S(2)}) copy-start(bf16[128,1024]{1,0:T(8,128)(2,1)} %param.11) | copy-start | bytes 786436
  6.5 36.4 %all-gather.3.cloned.1.call-start = ((), (), s32[]{:S(2)}) async-start(), calls=%async_computation.1 | async-start | bytes 1310720 | tf_op jit(solution)/shard_map/all_gather | solution.py:110
  7.4 5.6 %collective-permute-start = (bf16[2,3,1024]{2,0,1:T(2,128)(2,1)S(1)}, bf16[2,3,1024]{2,0,1:T(2,128)(2,1)S(1)}, u32[]{:S(2)}, u32[]{:S(2)}) collective-permute-start(bf16[2,3,1024]{2,0,1:T(2,128)(2,1)S(1)} %slice.38), channel_id=1, source_target_pairs={{0,4},{4,8},{8,12},{1,5},{5,9},{9,13},{2,6},{6,10},{10,14},{3,7},{... | collective-permute-start | bytes 36872 | tf_op jit(solution)/shard_map/ppermute | solution.py:15
  10.5 61.1 %all-gather.5.cloned.1.call-start = ((), (), s32[]{:S(2)}) async-start(), calls=%async_computation.2 | async-start | bytes 1310720 | tf_op jit(solution)/shard_map/all_gather | solution.py:111
  13.0 3.8 %copy-start.1 = (bf16[64,128]{1,0:T(8,128)(2,1)S(1)}, bf16[64,128]{1,0:T(8,128)(2,1)}, u32[]{:S(2)}) copy-start(bf16[64,128]{1,0:T(8,128)(2,1)} %param.9) | copy-start | bytes 49156
  15.5 22.4 %collective-permute-start.1 = (bf16[127,1024]{1,0:T(8,128)(2,1)S(1)}, bf16[127,1024]{1,0:T(8,128)(2,1)S(1)}, u32[]{:S(2)}, u32[]{:S(2)}) collective-permute-start(bf16[127,1024]{1,0:T(8,128)(2,1)S(1)} %slice_bitcast_fusion.1), channel_id=1, source_target_pairs={{0,4},{4,8},{8,12},{1,5},{5,9},{9,13},{2,6},{6,10},{10,14},{3,7},{... | collective-permute-start | bytes 780296 | tf_op jit(solution)/shard_map/ppermute | solution.py:15
  38.3 3.6 %copy-start.2 = (f32[1024]{0:T(1024)S(1)}, f32[1024]{0:T(1024)}, u32[]{:S(2)}) copy-start(f32[1024]{0:T(1024)} %param.10) | copy-start | bytes 12292
  42.8 62.5 %reduce-scatter.2.cloned.1.call-start = ((), (), s32[]{:S(2)}) async-start(), calls=%async_computation.3 | async-start | bytes 1310720 | tf_op jit(solution)/shard_map/reduce_scatter | solution.py:115
Sparse Core Ops, SparseCore 0:
  10.6 31.9 all-gather.2
  44.2 27.3 all-gather.4
  79.6 25.6 reduce-scatter.1
where the time goes:
time: 114 us; the launch traced here: 112 us
  waiting for transfers between devices  53.8 us (47%)
  local copies, waits for them, and re-layouts  25.7 us (23%)
  between operations  13.3 us (12%)
  matrix products  11.5 us (10%)
  other arithmetic  4.94 us (4%)
  starting transfers between devices  2.67 us (2%)
    all_gather x1, waiting for transfers between devices, per_device(): lax.all_gather(values, 'ctx', axis=0, tiled=True)  26.2 us
    reduce_scatter x1, waiting for transfers between devices, per_device(): lax.psum_scatter(partial_out.astype(jnp.bfloat16), 'mp', scatter_dimensio...  25.8 us
    reshape x1, local copies, waits for them, and re-layouts, toeplitz_taps(): return repeated[:, :row_count * span].reshape(group_count, row_count, span)  15.8 us
    dot_general x1, matrix products, per_device(): jnp.dot(attended, out_weight, preferred_element_type=jnp.float32)  5.65 us
    unnamed x8, local copies, waits for them, and re-layouts  4.4 us
    dot_general x1, matrix products, per_device(): jnp.einsum('gtr,rgc->tgc', toeplitz, gate_ext.reshape(row_count + tap_cou...  3.38 us
    ppermute x2, starting transfers between devices, passed_along(): lax.ppermute(value, axis, [(source, source + steps) for source in range(i...  2.58 us
    add x1, other arithmetic, short_features(): features + short_filter[lag_index].astype(jnp.float32)[None] * delayed  2.38 us
  transfers between devices with their start and end apart: 5, of which 3 were waited for; matrix products, arithmetic and copies ran while one was open for 30% of the time, Pallas kernels for 0%

commit v1 on v0

v1 whole, which is shorter than its diff:
```python
import functools

import jax
import jax.numpy as jnp
from jax import lax
from jax.experimental import pallas as pl
from jax.experimental.pallas import tpu as pltpu
from jax.sharding import PartitionSpec as P

HD = 128
MESH = pl.DeviceIdType.MESH
NEG = -1e30
F32 = jnp.float32
BF = jnp.bfloat16


def dot(a, b, ca=1, cb=0):
    return lax.dot_general(a, b, (((ca,), (cb,)), ((), ())), preferred_element_type=F32)


def kernel(
    n, m, x_hbm, sf_ref, lf_ref, skip_ref, q_hbm, k_hbm, w_hbm, out_ref,
    xb, rim_out, rim_in, f0, gown, gprev, taps, kbuf, vbuf, qbuf, mst, lst, ast,
    sbuf, sstat, pbuf, pstat, att, wv, acc, s1, r1, s2, r2,
    xsem, qsem, ksem, wsem, rim_s, rim_r, gate_s, gate_r, k_s, k_r, v_s, v_r,
    q_s, q_r, o_s, o_r, t_s, t_r, a_s, a_r, b_s, b_r,
):
    z = lax.axis_index("ctx")
    me = lax.axis_index("mp")
    core = lax.rem(me, 2)
    chip = me // 2
    chips = m // 2
    partner = chip * 2 + 1 - core
    pivot = n // 3
    slots = n - pivot
    rows = xb.shape[1]
    heads = gown.shape[0]
    groups = lf_ref.shape[0]
    per_tile = groups // heads
    width = HD // per_tile
    tap_count = lf_ref.shape[1]
    short = sf_ref.shape[0]
    span = min(3, slots) * rows
    query_groups = qbuf.shape[1] // span
    cols = out_ref.shape[1]
    own = jnp.minimum(z, pivot)

    def remote(src, dst, ss, rs, axis, target):
        return pltpu.make_async_remote_copy(
            src_ref=src, dst_ref=dst, send_sem=ss, recv_sem=rs,
            device_id={axis: target}, device_id_type=MESH)

    local_x = pltpu.make_async_copy(x_hbm, xb, xsem)
    local_x.start()
    local_k, local_q = [], []
    for h in range(heads):
        part = pl.ds(h * HD, HD)
        local_k.append(pltpu.make_async_copy(k_hbm.at[:, part], kbuf.at[own, h], ksem.at[h]))
        local_q.append(pltpu.make_async_copy(q_hbm.at[:, part], qbuf.at[h, pl.ds(0, rows)], qsem.at[h]))
    for c in local_k + local_q:
        c.start()
    local_w = pltpu.make_async_copy(w_hbm, wv, wsem)
    local_w.start()

    barrier = pltpu.get_barrier_semaphore()
    count = jnp.int32(m - 1)
    for other in range(m):
        @pl.when(other != me)
        def _():
            pl.semaphore_signal(barrier, inc=1, device_id={"mp": other}, device_id_type=MESH)
    for other in range(n):
        low, high = jnp.minimum(z, other), jnp.maximum(z, other)
        talks = (low != high) & ((high == low + 1) | (high <= pivot) | (low >= pivot))
        count = count + talks.astype(jnp.int32)

        @pl.when(talks)
        def _():
            pl.semaphore_signal(barrier, inc=1, device_id={"ctx": other}, device_id_type=MESH)

    local_x.wait()
    for j in range(3):
        rim_out[2 * j:2 * j + 2, :] = xb[j, rows - 2:rows, :]

    @pl.when(z == 0)
    def _():
        rim_in[...] = jnp.zeros_like(rim_in)
        gprev[...] = jnp.zeros_like(gprev)

    pl.semaphore_wait(barrier, count)

    up = jnp.minimum(z + 1, n - 1)
    rim = remote(rim_out, rim_in, rim_s, rim_r, "ctx", up)
    gate = remote(gown, gprev, gate_s, gate_r, "ctx", up)

    @pl.when(z < n - 1)
    def _():
        rim.start()

    for c in local_k + local_q:
        c.wait()

    def each_query(act):
        for other in range(pivot, n - 1):
            @pl.when(other < z)
            def _():
                act(remote(
                    qbuf.at[:, pl.ds(0, rows)],
                    qbuf.at[:, pl.ds(pl.multiple_of((z - other) * rows, rows), rows)],
                    q_s.at[other - pivot], q_r.at[z - other], "ctx", other))

    def each_key(act):
        for other in range(1, pivot + 1):
            @pl.when((other > z) & (z < pivot))
            def _():
                act(remote(kbuf.at[own], kbuf.at[own], k_s.at[other], k_r.at[own], "ctx", other))

    def each_value(h, act):
        for other in range(1, pivot + 1):
            @pl.when((other > z) & (z < pivot))
            def _():
                act(remote(vbuf.at[own, h], vbuf.at[own, h], v_s.at[other, h], v_r.at[own, h], "ctx", other))

    each_query(lambda c: c.start())
    each_key(lambda c: c.start())

    @pl.when(z > 0)
    def _():
        rim.wait_recv()

    row = lax.broadcasted_iota(jnp.int32, (rows, HD), 0)

    @pl.loop(0, heads)
    def _(h):
        part = pl.ds(pl.multiple_of(h * HD, HD), HD)
        edge = rim_in[:, part].astype(F32)
        feats = []
        for j in range(3):
            x = xb[j, :, part].astype(F32)
            last = edge[2 * j + 1:2 * j + 2]
            x1 = jnp.where(row == 0, last, pltpu.roll(x, 1, 0))
            x2 = jnp.where(row == 0, edge[2 * j:2 * j + 1],
                           jnp.where(row == 1, last, pltpu.roll(x, 2, 0)))
            total = sf_ref[0, j:j + 1, part].astype(F32) * x
            total = total + sf_ref[1, j:j + 1, part].astype(F32) * x1
            feats.append(total + sf_ref[2, j:j + 1, part].astype(F32) * x2)
        f0[h] = feats[0]
        gown[h] = (feats[1] * feats[2]).astype(BF)

    @pl.when(z < n - 1)
    def _():
        gate.start()

    flip = (lax.broadcasted_iota(jnp.int32, (tap_count, 2 * rows), 0)
            + lax.broadcasted_iota(jnp.int32, (tap_count, 2 * rows), 1)) == rows
    based = dot(lf_ref[...], flip.astype(BF))
    for g in range(groups):
        wide = jnp.broadcast_to(based[g:g + 1], (rows, 2 * rows))
        taps[g] = pltpu.roll(wide, 0, 1, stride=1, stride_axis=0).astype(BF)
    acc[...] = jnp.zeros_like(acc)

    @pl.when(z > 0)
    def _():
        gate.wait_recv()

    lane = lax.broadcasted_iota(jnp.int32, (rows, HD), 1) // width

    @pl.loop(0, heads)
    def _(h):
        mine = gown[h]
        both = jnp.concatenate([gprev[h], mine], axis=0)
        filt = jnp.zeros((rows, HD), F32)
        for g in range(per_tile):
            filt = jnp.where(lane == g, dot(taps[h * per_tile + g], both), filt)
        part = pl.ds(pl.multiple_of(h * HD, HD), HD)
        val = f0[h] * (filt + skip_ref[:, part] * mine.astype(F32))
        vbuf[own, h] = val.T.astype(BF)
        each_value(h, lambda c: c.start())

    scale = HD ** -0.5
    krow = lax.broadcasted_iota(jnp.int32, (rows, span), 0)
    kcol = lax.broadcasted_iota(jnp.int32, (rows, span), 1)

    def each_part(h, act):
        for s in range(1, slots):
            @pl.when((z >= pivot) & (z + s < n))
            def _():
                act(s,
                    remote(sbuf.at[s - 1, h], pbuf.at[z - pivot, h],
                           o_s.at[s - 1, h], o_r.at[z - pivot, h], "ctx", z + s),
                    remote(sstat.at[s - 1, h], pstat.at[z - pivot, h],
                           t_s.at[s - 1, h], t_r.at[z - pivot, h], "ctx", z + s))

    def hand_over(h):
        def act(s, o, t):
            gi, at = (s * rows) // span, (s * rows) % span
            mm = mst[h, gi, :, at:at + rows]
            ll = lst[h, gi, :, at:at + rows]
            aa = ast[h, gi, :, at:at + rows]
            sbuf[s - 1, h] = (aa * (1.0 / ll[0:1])).astype(BF)
            sstat[s - 1, h] = mm + jnp.log(ll)
            o.start()
            t.start()
        each_part(h, act)

    for s in range(1, slots):
        @pl.when((z >= pivot) & (z + s < n))
        def _():
            pltpu.make_async_remote_copy(
                src_ref=qbuf.at[:, pl.ds(0, rows)], dst_ref=qbuf.at[:, pl.ds(s * rows, rows)],
                send_sem=q_s.at[0], recv_sem=q_r.at[s],
                device_id={"ctx": jnp.minimum(z + s, n - 1)}, device_id_type=MESH).wait_recv()

    @pl.loop(0, heads)
    def _(h):
        for gi in range(query_groups):
            q = qbuf[h, gi * span:(gi + 1) * span]
            s = dot(kbuf[own, h], q, 1, 1) * scale
            s = jnp.where(krow <= kcol + gi * span, s, NEG)
            mx = jnp.max(s, axis=0, keepdims=True)
            p = jnp.exp(s - mx)
            mst[h, gi] = jnp.broadcast_to(mx, (8, span))
            lst[h, gi] = jnp.broadcast_to(jnp.sum(p, axis=0, keepdims=True), (8, span))
            ast[h, gi] = dot(vbuf[own, h], p.astype(BF))

        @pl.when(z > pivot)
        def _():
            hand_over(h)

    @pl.when((z > 0) & (z <= pivot))
    def _():
        @pl.loop(0, z)
        def _(j):
            remote(kbuf.at[j], kbuf.at[j], k_s.at[0], k_r.at[j], "ctx", j).wait_recv()

    def one_head(h):
        @pl.loop(0, jnp.where(z <= pivot, z, 0))
        def _(j):
            remote(vbuf.at[j, h], vbuf.at[j, h], v_s.at[0, 0], v_r.at[j, h], "ctx", j).wait_recv()
            for gi in range(query_groups):
                q = qbuf[h, gi * span:(gi + 1) * span]
                s = dot(kbuf[j, h], q, 1, 1) * scale
                old = mst[h, gi, 0:1]
                mx = jnp.maximum(old, jnp.max(s, axis=0, keepdims=True))
                p = jnp.exp(s - mx)
                fade = jnp.exp(old - mx)
                mst[h, gi] = jnp.broadcast_to(mx, (8, span))
                lst[h, gi] = jnp.broadcast_to(
                    lst[h, gi, 0:1] * fade + jnp.sum(p, axis=0, keepdims=True), (8, span))
                ast[h, gi] = ast[h, gi] * fade + dot(vbuf[j, h], p.astype(BF))

        @pl.when(z == pivot)
        def _():
            hand_over(h)

        @pl.loop(0, jnp.maximum(z - pivot, 0))
        def _(j):
            remote(sbuf.at[0, 0], pbuf.at[j, h], o_s.at[0, 0], o_r.at[j, h], "ctx", j + pivot).wait_recv()
            remote(sstat.at[0, 0], pstat.at[j, h], t_s.at[0, 0], t_r.at[j, h], "ctx", j + pivot).wait_recv()
            old = mst[h, 0, :, 0:rows]
            lse = pstat[j, h]
            mx = jnp.maximum(old, lse)
            fade, gain = jnp.exp(old - mx), jnp.exp(lse - mx)
            mst[h, 0, :, 0:rows] = mx
            lst[h, 0, :, 0:rows] = lst[h, 0, :, 0:rows] * fade + gain
            ast[h, 0, :, 0:rows] = ast[h, 0, :, 0:rows] * fade[0:1] + pbuf[j, h].astype(F32) * gain[0:1]

        done = ast[h, 0, :, 0:rows] * (1.0 / lst[h, 0, 0:1, 0:rows])
        return done.T.astype(BF)

    @pl.loop(0, heads // 2)
    def _(c):
        att[c, :, 0:HD] = one_head(2 * c)
        att[c, :, HD:2 * HD] = one_head(2 * c + 1)

        @pl.when(c == 0)
        def _():
            local_w.wait()

        lhs = att[c]

        @pl.loop(0, m)
        def _(b):
            at = pl.ds(pl.multiple_of(b * cols, cols), cols)
            acc[b] += dot(lhs, wv[pl.ds(pl.multiple_of(c * 2 * HD, 2 * HD), 2 * HD), at])

    pieces = 4
    piece = cols // pieces

    def across(d, i):
        return remote(s1.at[d, i], r1.at[d, i], a_s.at[d, i], a_r.at[d, i], "mp", partner)

    def along(d, i):
        there = lax.rem(chip + d, chips) * 2 + core
        return remote(s2.at[d, i], r2.at[d, i], b_s.at[d, i], b_r.at[d, i], "mp", there)

    order = [d % chips for d in range(1, chips + 1)]
    for d in order:
        b = lax.rem(chip + d, chips) * 2 + 1 - core
        for i in range(pieces):
            s1[d, i] = acc[b, :, i * piece:(i + 1) * piece].astype(BF)
            across(d, i).start()
    for d in range(1, chips):
        b = lax.rem(chip + d, chips) * 2 + core
        for i in range(pieces):
            across(d, i).wait_recv()
            s2[d, i] = (acc[b, :, i * piece:(i + 1) * piece] + r1[d, i].astype(F32)).astype(BF)
            along(d, i).start()
    for i in range(pieces):
        across(0, i).wait_recv()
        total = acc[me, :, i * piece:(i + 1) * piece] + r1[0, i].astype(F32)
        for d in range(1, chips):
            along(d, i).wait_recv()
            total = total + r2[d, i].astype(F32)
        out_ref[:, i * piece:(i + 1) * piece] = total.astype(BF)

    for i in range(pieces):
        for d in range(chips):
            across(d, i).wait_send()
        for d in range(1, chips):
            along(d, i).wait_send()

    @pl.when(z < n - 1)
    def _():
        rim.wait_send()
        gate.wait_send()

    each_query(lambda c: c.wait_send())
    each_key(lambda c: c.wait_send())

    @pl.loop(0, heads)
    def _(h):
        def ended(s, o, t):
            o.wait_send()
            t.wait_send()
        each_value(h, lambda c: c.wait_send())
        each_part(h, ended)


def per_device(n, m, inputs, short_filter, long_filter, skip_gain, queries, key_rows, out_weight):
    rows, _, channels = inputs.shape
    heads = channels // HD
    groups = long_filter.shape[0]
    total = out_weight.shape[1]
    cols = total // m
    chips = m // 2
    pivot = n // 3
    slots = n - pivot
    batch = min(3, slots)
    padded = -(-slots // batch) * batch
    span = batch * rows
    gq = padded // batch
    parts = max(slots - 1, 1)
    vm = pltpu.VMEM
    dma = pltpu.SemaphoreType.DMA
    scratch = [
        vm((3, rows, channels), BF), vm((16, channels), BF), vm((16, channels), BF),
        vm((heads, rows, HD), F32), vm((heads, rows, HD), BF), vm((heads, rows, HD), BF),
        vm((groups, rows, 2 * rows), BF),
        vm((pivot + 1, heads, rows, HD), BF), vm((pivot + 1, heads, HD, rows), BF),
        vm((heads, padded * rows, HD), BF),
        vm((heads, gq, 8, span), F32), vm((heads, gq, 8, span), F32), vm((heads, gq, HD, span), F32),
        vm((parts, heads, HD, rows), BF), vm((parts, heads, 8, rows), F32),
        vm((parts, heads, HD, rows), BF), vm((parts, heads, 8, rows), F32),
        vm((heads // 2, rows, 2 * HD), BF), vm((channels, total), BF), vm((m, rows, cols), F32),
    ] + [vm((chips, 4, rows, cols // 4), BF)] * 4 + [
        dma, dma((heads,)), dma((heads,)), dma, dma, dma, dma, dma,
        dma((pivot + 1,)), dma((pivot + 1,)), dma((pivot + 1, heads)), dma((pivot + 1, heads)),
        dma((slots,)), dma((slots,)),
        dma((parts, heads)), dma((parts, heads)), dma((parts, heads)), dma((parts, heads)),
    ] + [dma((chips, 4))] * 4
    in_vmem = pl.BlockSpec(memory_space=pltpu.VMEM)
    in_hbm = pl.BlockSpec(memory_space=pl.ANY)
    return pl.pallas_call(
        functools.partial(kernel, n, m),
        out_shape=jax.ShapeDtypeStruct((rows, cols), BF),
        in_specs=[in_hbm, in_vmem, in_vmem, in_vmem, in_hbm, in_hbm, in_hbm],
        out_specs=in_vmem,
        scratch_shapes=scratch,
        compiler_params=pltpu.CompilerParams(
            collective_id=0, has_side_effects=True, vmem_limit_bytes=60 * 2**20),
    )(inputs.transpose(1, 0, 2), short_filter, long_filter, skip_gain[None], queries, key_rows, out_weight)


def solution(mesh):
    placed = (
        P(("parts", "ctx"), None, "mp"),
        P(None, None, "mp"),
        P("mp", None),
        P("mp"),
        P(("parts", "ctx"), "mp"),
        P(("parts", "ctx"), "mp"),
        P("mp", None),
    )
    return jax.shard_map(
        functools.partial(per_device, mesh.shape["ctx"], mesh.shape["mp"]),
        mesh=mesh, in_specs=placed, out_specs=P(("parts", "ctx"), "mp"), check_vma=False)
```

time: 114 us -> 49.1 us (0.43); the launches traced: 112 us -> 48.3 us
  waiting for transfers between devices: 53.8 us -> 0 us
  Pallas kernels: 0 us -> 46.7 us
  local copies, waits for them, and re-layouts: 25.7 us -> 1.67 us
  between operations: 13.3 us -> 0.01 us
  matrix products: 11.5 us -> 0 us
  other arithmetic: 4.94 us -> 0 us
  starting transfers between devices: 2.67 us -> 0 us
    pallas_call x0 -> x1, Pallas kernels: none -> 46.7 us  [per_device(): pl.pallas_call(functools.partial(kernel, n, m), out_shape=jax.ShapeDtypeS...]
    all_gather x2 -> x0, waiting for transfers between devices: 26.2 us -> none  [the longest x1 26.2 us: per_device(): lax.all_gather(values, 'ctx', axis=0, tiled=True)]
    reduce_scatter x1 -> x0, waiting for transfers between devices: 25.8 us -> none  [per_device(): lax.psum_scatter(partial_out.astype(jnp.bfloat16), 'mp', scatter_dimensio...]
    reshape x2 -> x0, local copies, waits for them, and re-layouts: 16.1 us -> none  [the longest x1 15.8 us: toeplitz_taps(): return repeated[:, :row_count * span].reshape(group_count, row_count, span)]
    dot_general x4 -> x0, matrix products: 11.5 us -> none  [the longest x1 5.65 us: per_device(): jnp.dot(attended, out_weight, preferred_element_type=jnp.float32)]
    slice x3 -> x0, local copies, waits for them, and re-layouts: 3.16 us -> none  [the longest x1 2.24 us: toeplitz_taps(): return repeated[:, :row_count * span].reshape(group_count, row_count, span)]
    unnamed x8 -> x1, local copies, waits for them, and re-layouts: 4.4 us -> 1.67 us
    ppermute x2 -> x0, starting transfers between devices: 2.58 us -> none  [passed_along(): lax.ppermute(value, axis, [(source, source + steps) for source in range(i...]
  transfers between devices with their start and end apart: 5 -> 0, of which waited for: 3 -> 0; matrix products, arithmetic and copies ran while one was open for 30% -> 0% of each run, Pallas kernels for 0% -> 0%
where the time goes in v1:
time: 49.1 us; the launch traced here: 48.3 us
  Pallas kernels  46.7 us (95%)
  local copies, waits for them, and re-layouts  1.67 us (3%)
    pallas_call x1, Pallas kernels, per_device(): pl.pallas_call(functools.partial(kernel, n, m), out_shape=jax.ShapeDtypeS...  46.7 us
    unnamed x1, local copies, waits for them, and re-layouts  1.67 us

profile of v1, /device:TPU:28, one launch (start us, length us, event | category | flops | bytes accessed | tf_op | source)
XLA Modules:
  0.0 48.3 jit_solution(17304952185844223028)
XLA Ops:
  0.0 46.7 %shard_map.73 = bf16[128,1024]{1,0:T(8,128)(2,1)} custom-call(bf16[3,128,1024]{2,1,0:T(8,128)(2,1)} %bitcast.2, bf16[3,3,1024]{2,1,0:T(4,128)(2,1)} %sf_ref.1, bf16[64,128]{1,0:T(8,128)(2,1)} %lf_ref.1, f32[1,1024]{1,0:T(1,128)} %bitcast.3, bf16[128,1024]{1,0:T(8,128)(2,1)} %q_hbm.1, bf16[128,1024]{1,0:T(8,128)(2,1)} %k_hbm.1, bf16[1024,4096]{1,0:T(8,128)(2,1)} %w_hbm.1), custom_call_target="tpu_custom_call" | custom-call | tf_op jit(solution)/shard_map/pallas_call | solution.py:373
  46.7 1.7 %copy.9 = bf16[128,1024]{1,0:T(8,128)(2,1)} copy(bf16[128,1024]{1,0:T(8,128)(2,1)} %shard_map.73) | data formatting | bytes 524288

commit v2 on v1

--- a/solution.py
+++ b/solution.py
@@ -43,6 +43,7 @@
     span = min(3, slots) * rows
     query_groups = qbuf.shape[1] // span
     cols = out_ref.shape[1]
+    channels = xb.shape[2]
     own = jnp.minimum(z, pivot)
 
     def remote(src, dst, ss, rs, axis, target):
@@ -90,7 +91,9 @@
 
     up = jnp.minimum(z + 1, n - 1)
     rim = remote(rim_out, rim_in, rim_s, rim_r, "ctx", up)
-    gate = remote(gown, gprev, gate_s, gate_r, "ctx", up)
+
+    def gate(h):
+        return remote(gown.at[h], gprev.at[h], gate_s.at[h], gate_r.at[h], "ctx", up)
 
     @pl.when(z < n - 1)
     def _():
@@ -99,20 +102,20 @@
     for c in local_k + local_q:
         c.wait()
 
-    def each_query(act):
+    def each_query(h, act):
         for other in range(pivot, n - 1):
             @pl.when(other < z)
             def _():
                 act(remote(
-                    qbuf.at[:, pl.ds(0, rows)],
-                    qbuf.at[:, pl.ds(pl.multiple_of((z - other) * rows, rows), rows)],
-                    q_s.at[other - pivot], q_r.at[z - other], "ctx", other))
-
-    def each_key(act):
+                    qbuf.at[h, pl.ds(0, rows)],
+                    qbuf.at[h, pl.ds(pl.multiple_of((z - other) * rows, rows), rows)],
+                    q_s.at[other - pivot, h], q_r.at[z - other, h], "ctx", other))
+
+    def each_key(h, act):
         for other in range(1, pivot + 1):
             @pl.when((other > z) & (z < pivot))
             def _():
-                act(remote(kbuf.at[own], kbuf.at[own], k_s.at[other], k_r.at[own], "ctx", other))
+                act(remote(kbuf.at[own, h], kbuf.at[own, h], k_s.at[other, h], k_r.at[own, h], "ctx", other))
 
     def each_value(h, act):
         for other in range(1, pivot + 1):
@@ -120,8 +123,13 @@
             def _():
                 act(remote(vbuf.at[own, h], vbuf.at[own, h], v_s.at[other, h], v_r.at[own, h], "ctx", other))
 
-    each_query(lambda c: c.start())
-    each_key(lambda c: c.start())
+    early = min(2, heads)
+    for h in range(early):
+        each_key(h, lambda c: c.start())
+
+    @pl.loop(0, heads)
+    def _(h):
+        each_query(h, lambda c: c.start())
 
     @pl.when(z > 0)
     def _():
@@ -146,9 +154,9 @@
         f0[h] = feats[0]
         gown[h] = (feats[1] * feats[2]).astype(BF)
 
-    @pl.when(z < n - 1)
-    def _():
-        gate.start()
+        @pl.when(z < n - 1)
+        def _():
+            gate(h).start()
 
     flip = (lax.broadcasted_iota(jnp.int32, (tap_count, 2 * rows), 0)
             + lax.broadcasted_iota(jnp.int32, (tap_count, 2 * rows), 1)) == rows
@@ -158,14 +166,14 @@
         taps[g] = pltpu.roll(wide, 0, 1, stride=1, stride_axis=0).astype(BF)
     acc[...] = jnp.zeros_like(acc)
 
-    @pl.when(z > 0)
-    def _():
-        gate.wait_recv()
-
     lane = lax.broadcasted_iota(jnp.int32, (rows, HD), 1) // width
 
     @pl.loop(0, heads)
     def _(h):
+        @pl.when(z > 0)
+        def _():
+            gate(h).wait_recv()
+
         mine = gown[h]
         both = jnp.concatenate([gprev[h], mine], axis=0)
         filt = jnp.zeros((rows, HD), F32)
@@ -174,6 +182,11 @@
         part = pl.ds(pl.multiple_of(h * HD, HD), HD)
         val = f0[h] * (filt + skip_ref[:, part] * mine.astype(F32))
         vbuf[own, h] = val.T.astype(BF)
+
+        @pl.when(h >= early)
+        def _():
+            each_key(h, lambda c: c.start())
+
         each_value(h, lambda c: c.start())
 
     scale = HD ** -0.5
@@ -202,16 +215,13 @@
             t.start()
         each_part(h, act)
 
-    for s in range(1, slots):
-        @pl.when((z >= pivot) & (z + s < n))
-        def _():
-            pltpu.make_async_remote_copy(
-                src_ref=qbuf.at[:, pl.ds(0, rows)], dst_ref=qbuf.at[:, pl.ds(s * rows, rows)],
-                send_sem=q_s.at[0], recv_sem=q_r.at[s],
-                device_id={"ctx": jnp.minimum(z + s, n - 1)}, device_id_type=MESH).wait_recv()
-
-    @pl.loop(0, heads)
-    def _(h):
+    def own_keys(h):
+        for s in range(1, slots):
+            @pl.when((z >= pivot) & (z + s < n))
+            def _():
+                remote(qbuf.at[h, pl.ds(0, rows)], qbuf.at[h, pl.ds(s * rows, rows)],
+                       q_s.at[0, h], q_r.at[s, h], "ctx", jnp.minimum(z + s, n - 1)).wait_recv()
+
         for gi in range(query_groups):
             q = qbuf[h, gi * span:(gi + 1) * span]
             s = dot(kbuf[own, h], q, 1, 1) * scale
@@ -222,19 +232,21 @@
             lst[h, gi] = jnp.broadcast_to(jnp.sum(p, axis=0, keepdims=True), (8, span))
             ast[h, gi] = dot(vbuf[own, h], p.astype(BF))
 
-        @pl.when(z > pivot)
-        def _():
+    @pl.when(z > pivot)
+    def _():
+        @pl.loop(0, heads)
+        def _(h):
+            own_keys(h)
             hand_over(h)
 
-    @pl.when((z > 0) & (z <= pivot))
-    def _():
-        @pl.loop(0, z)
-        def _(j):
-            remote(kbuf.at[j], kbuf.at[j], k_s.at[0], k_r.at[j], "ctx", j).wait_recv()
-
     def one_head(h):
+        @pl.when(z <= pivot)
+        def _():
+            own_keys(h)
+
         @pl.loop(0, jnp.where(z <= pivot, z, 0))
         def _(j):
+            remote(kbuf.at[j, h], kbuf.at[j, h], k_s.at[0, 0], k_r.at[j, h], "ctx", j).wait_recv()
             remote(vbuf.at[j, h], vbuf.at[j, h], v_s.at[0, 0], v_r.at[j, h], "ctx", j).wait_recv()
             for gi in range(query_groups):
                 q = qbuf[h, gi * span:(gi + 1) * span]
@@ -276,12 +288,14 @@
         def _():
             local_w.wait()
 
-        lhs = att[c]
-
-        @pl.loop(0, m)
-        def _(b):
-            at = pl.ds(pl.multiple_of(b * cols, cols), cols)
-            acc[b] += dot(lhs, wv[pl.ds(pl.multiple_of(c * 2 * HD, 2 * HD), 2 * HD), at])
+        @pl.when(c < heads // 2 - 1)
+        def _():
+            lhs = att[c]
+
+            @pl.loop(0, m)
+            def _(b):
+                at = pl.ds(pl.multiple_of(b * cols, cols), cols)
+                acc[b] += dot(lhs, wv[pl.ds(pl.multiple_of(c * 2 * HD, 2 * HD), 2 * HD), at])
 
     pieces = 4
     piece = cols // pieces
@@ -293,21 +307,33 @@
         there = lax.rem(chip + d, chips) * 2 + core
         return remote(s2.at[d, i], r2.at[d, i], b_s.at[d, i], b_r.at[d, i], "mp", there)
 
+    last = att[heads // 2 - 1]
+
+    def summed(b, i):
+        at = pl.ds(pl.multiple_of(b * cols + i * piece, piece), piece)
+        return acc[b, :, i * piece:(i + 1) * piece] + dot(last, wv[channels - 2 * HD:, at])
+
+    def block(d, side):
+        return lax.rem(chip + d, chips) * 2 + side
+
     order = [d % chips for d in range(1, chips + 1)]
     for d in order:
-        b = lax.rem(chip + d, chips) * 2 + 1 - core
         for i in range(pieces):
-            s1[d, i] = acc[b, :, i * piece:(i + 1) * piece].astype(BF)
+            s1[d, i] = summed(block(d, 1 - core), i).astype(BF)
             across(d, i).start()
     for d in range(1, chips):
-        b = lax.rem(chip + d, chips) * 2 + core
         for i in range(pieces):
+            total = summed(block(d, core), i)
             across(d, i).wait_recv()
-            s2[d, i] = (acc[b, :, i * piece:(i + 1) * piece] + r1[d, i].astype(F32)).astype(BF)
+            s2[d, i] = (total + r1[d, i].astype(F32)).astype(BF)
             along(d, i).start()
     for i in range(pieces):
+        acc[me, :, i * piece:(i + 1) * piece] = summed(me, i)
+    for i in range(pieces):
         across(0, i).wait_recv()
-        total = acc[me, :, i * piece:(i + 1) * piece] + r1[0, i].astype(F32)
+        acc[me, :, i * piece:(i + 1) * piece] += r1[0, i].astype(F32)
+    for i in range(pieces):
+        total = acc[me, :, i * piece:(i + 1) * piece]
         for d in range(1, chips):
             along(d, i).wait_recv()
             total = total + r2[d, i].astype(F32)
@@ -322,16 +348,18 @@
     @pl.when(z < n - 1)
     def _():
         rim.wait_send()
-        gate.wait_send()
-
-    each_query(lambda c: c.wait_send())
-    each_key(lambda c: c.wait_send())
 
     @pl.loop(0, heads)
     def _(h):
         def ended(s, o, t):
             o.wait_send()
             t.wait_send()
+        @pl.when(z < n - 1)
+        def _():
+            gate(h).wait_send()
+
+        each_query(h, lambda c: c.wait_send())
+        each_key(h, lambda c: c.wait_send())
         each_value(h, lambda c: c.wait_send())
         each_part(h, ended)
 
@@ -363,9 +391,8 @@
         vm((parts, heads, HD, rows), BF), vm((parts, heads, 8, rows), F32),
         vm((heads // 2, rows, 2 * HD), BF), vm((channels, total), BF), vm((m, rows, cols), F32),
     ] + [vm((chips, 4, rows, cols // 4), BF)] * 4 + [
-        dma, dma((heads,)), dma((heads,)), dma, dma, dma, dma, dma,
-        dma((pivot + 1,)), dma((pivot + 1,)), dma((pivot + 1, heads)), dma((pivot + 1, heads)),
-        dma((slots,)), dma((slots,)),
+        dma, dma((heads,)), dma((heads,)), dma, dma, dma, dma((heads,)), dma((heads,)),
+    ] + [dma((pivot + 1, heads))] * 4 + [dma((slots, heads))] * 2 + [
         dma((parts, heads)), dma((parts, heads)), dma((parts, heads)), dma((parts, heads)),
     ] + [dma((chips, 4))] * 4
     in_vmem = pl.BlockSpec(memory_space=pltpu.VMEM)

time: 49.1 us -> 40.8 us (0.83); the launches traced: 48.3 us -> 40.5 us
  Pallas kernels: 46.7 us -> 38.9 us
    pallas_call x1, Pallas kernels: 46.7 us -> 38.9 us  [per_device(): pl.pallas_call(functools.partial(kernel, n, m), out_shape=jax.ShapeDtypeS...]
where the time goes in v2:
time: 40.8 us; the launch traced here: 40.5 us
  Pallas kernels  38.9 us (95%)
  local copies, waits for them, and re-layouts  1.67 us (4%)
    pallas_call x1, Pallas kernels, per_device(): pl.pallas_call(functools.partial(kernel, n, m), out_shape=jax.ShapeDtypeS...  38.9 us
    unnamed x1, local copies, waits for them, and re-layouts  1.67 us

profile of v2, /device:TPU:28, one launch (start us, length us, event | category | flops | bytes accessed | tf_op | source)
XLA Modules:
  0.0 40.5 jit_solution(13414021276489288307)
XLA Ops:
  0.0 38.9 %shard_map.73 = bf16[128,1024]{1,0:T(8,128)(2,1)} custom-call(bf16[3,128,1024]{2,1,0:T(8,128)(2,1)} %bitcast.2, bf16[3,3,1024]{2,1,0:T(4,128)(2,1)} %sf_ref.1, bf16[64,128]{1,0:T(8,128)(2,1)} %lf_ref.1, f32[1,1024]{1,0:T(1,128)} %bitcast.3, bf16[128,1024]{1,0:T(8,128)(2,1)} %q_hbm.1, bf16[128,1024]{1,0:T(8,128)(2,1)} %k_hbm.1, bf16[1024,4096]{1,0:T(8,128)(2,1)} %w_hbm.1), custom_call_target="tpu_custom_call" | custom-call | tf_op jit(solution)/shard_map/pallas_call | solution.py:400
  38.9 1.7 %copy.9 = bf16[128,1024]{1,0:T(8,128)(2,1)} copy(bf16[128,1024]{1,0:T(8,128)(2,1)} %shard_map.73) | data formatting | bytes 524288

commit v3 on v2

--- a/solution.py
+++ b/solution.py
@@ -19,8 +19,8 @@
 
 
 def kernel(
-    n, m, x_hbm, sf_ref, lf_ref, skip_ref, q_hbm, k_hbm, w_hbm, out_ref,
-    xb, rim_out, rim_in, f0, gown, gprev, taps, kbuf, vbuf, qbuf, mst, lst, ast,
+    n, m, x_hbm, sf_hbm, lf_hbm, skip_hbm, q_hbm, k_hbm, w_hbm, out_ref,
+    sf_ref, lf_ref, skip_ref, psem, xb, rim_out, rim_in, f0, gown, gprev, taps, kbuf, vbuf, qbuf, mst, lst, ast,
     sbuf, sstat, pbuf, pstat, att, wv, acc, s1, r1, s2, r2,
     xsem, qsem, ksem, wsem, rim_s, rim_r, gate_s, gate_r, k_s, k_r, v_s, v_r,
     q_s, q_r, o_s, o_r, t_s, t_r, a_s, a_r, b_s, b_r,
@@ -51,8 +51,27 @@
             src_ref=src, dst_ref=dst, send_sem=ss, recv_sem=rs,
             device_id={axis: target}, device_id_type=MESH)
 
+    barrier = pltpu.get_barrier_semaphore()
+    count = jnp.int32(m - 1)
+    for other in range(m):
+        @pl.when(other != me)
+        def _():
+            pl.semaphore_signal(barrier, inc=1, device_id={"mp": other}, device_id_type=MESH)
+    for other in range(n):
+        low, high = jnp.minimum(z, other), jnp.maximum(z, other)
+        talks = (low != high) & ((high == low + 1) | (high <= pivot) | (low >= pivot))
+        count = count + talks.astype(jnp.int32)
+
+        @pl.when(talks)
+        def _():
+            pl.semaphore_signal(barrier, inc=1, device_id={"ctx": other}, device_id_type=MESH)
+
     local_x = pltpu.make_async_copy(x_hbm, xb, xsem)
     local_x.start()
+    small = [pltpu.make_async_copy(a, b, psem.at[i]) for i, (a, b) in enumerate(
+        ((sf_hbm, sf_ref), (lf_hbm, lf_ref), (skip_hbm, skip_ref)))]
+    for c in small:
+        c.start()
     local_k, local_q = [], []
     for h in range(heads):
         part = pl.ds(h * HD, HD)
@@ -63,21 +82,6 @@
     local_w = pltpu.make_async_copy(w_hbm, wv, wsem)
     local_w.start()
 
-    barrier = pltpu.get_barrier_semaphore()
-    count = jnp.int32(m - 1)
-    for other in range(m):
-        @pl.when(other != me)
-        def _():
-            pl.semaphore_signal(barrier, inc=1, device_id={"mp": other}, device_id_type=MESH)
-    for other in range(n):
-        low, high = jnp.minimum(z, other), jnp.maximum(z, other)
-        talks = (low != high) & ((high == low + 1) | (high <= pivot) | (low >= pivot))
-        count = count + talks.astype(jnp.int32)
-
-        @pl.when(talks)
-        def _():
-            pl.semaphore_signal(barrier, inc=1, device_id={"ctx": other}, device_id_type=MESH)
-
     local_x.wait()
     for j in range(3):
         rim_out[2 * j:2 * j + 2, :] = xb[j, rows - 2:rows, :]
@@ -135,6 +139,8 @@
     def _():
         rim.wait_recv()
 
+    for c in small:
+        c.wait()
     row = lax.broadcasted_iota(jnp.int32, (rows, HD), 0)
 
     @pl.loop(0, heads)
@@ -381,6 +387,7 @@
     vm = pltpu.VMEM
     dma = pltpu.SemaphoreType.DMA
     scratch = [
+        vm(short_filter.shape, BF), vm(long_filter.shape, BF), vm((1, channels), F32), dma((3,)),
         vm((3, rows, channels), BF), vm((16, channels), BF), vm((16, channels), BF),
         vm((heads, rows, HD), F32), vm((heads, rows, HD), BF), vm((heads, rows, HD), BF),
         vm((groups, rows, 2 * rows), BF),
@@ -399,8 +406,8 @@
     in_hbm = pl.BlockSpec(memory_space=pl.ANY)
     return pl.pallas_call(
         functools.partial(kernel, n, m),
-        out_shape=jax.ShapeDtypeStruct((rows, cols), BF),
-        in_specs=[in_hbm, in_vmem, in_vmem, in_vmem, in_hbm, in_hbm, in_hbm],
+        out_shape=pltpu.VMEM((rows, cols), BF),
+        in_specs=[in_hbm] * 7,
         out_specs=in_vmem,
         scratch_shapes=scratch,
         compiler_params=pltpu.CompilerParams(

time: 40.8 us -> 38.2 us (0.936)
  Pallas kernels: 38.9 us -> 37.4 us
  local copies, waits for them, and re-layouts: 1.67 us -> 0.71 us
    pallas_call x1, Pallas kernels: 38.9 us -> 37.4 us  [per_device(): pl.pallas_call(functools.partial(kernel, n, m), out_shape=pltpu.VMEM((row...]
    unnamed x1, local copies, waits for them, and re-layouts: 1.67 us -> 0.71 us
where the time goes in v3:
time: 38.2 us; the launch traced here: 38.1 us
  Pallas kernels  37.4 us (98%)
  local copies, waits for them, and re-layouts  0.71 us (2%)
    pallas_call x1, Pallas kernels, per_device(): pl.pallas_call(functools.partial(kernel, n, m), out_shape=pltpu.VMEM((row...  37.4 us

profile of v3, /device:TPU:28, one launch (start us, length us, event | category | flops | bytes accessed | tf_op | source)
XLA Modules:
  0.0 38.1 jit_solution(2218170024390831931)
XLA Ops:
  0.0 37.4 %shard_map.73 = bf16[128,1024]{1,0:T(8,128)(2,1)S(1)} custom-call(bf16[3,128,1024]{2,1,0:T(8,128)(2,1)} %bitcast.2, bf16[3,3,1024]{2,1,0:T(4,128)(2,1)} %sf_hbm.1, bf16[64,128]{1,0:T(8,128)(2,1)} %lf_hbm.1, f32[1,1024]{1,0:T(1,128)} %bitcast.3, bf16[128,1024]{1,0:T(8,128)(2,1)} %q_hbm.1, bf16[128,1024]{1,0:T(8,128)(2,1)} %k_hbm.1, bf16[1024,4096]{1,0:T(8,128)(2,1)} %w_hbm.1), custom_call_target="tpu_custom_call" | custom-call | tf_op jit(solution)/shard_map/pallas_call | solution.py:407
  37.4 0.7 %copy.9 = bf16[128,1024]{1,0:T(8,128)(2,1)} copy(bf16[128,1024]{1,0:T(8,128)(2,1)S(1)} %shard_map.73) | data formatting | bytes 524288

commit v4 on v3

--- a/solution.py
+++ b/solution.py
@@ -128,6 +128,7 @@
                 act(remote(vbuf.at[own, h], vbuf.at[own, h], v_s.at[other, h], v_r.at[own, h], "ctx", other))
 
     early = min(2, heads)
+    ahead = min(4, heads)
     for h in range(early):
         each_key(h, lambda c: c.start())
 
@@ -160,7 +161,7 @@
         f0[h] = feats[0]
         gown[h] = (feats[1] * feats[2]).astype(BF)
 
-        @pl.when(z < n - 1)
+        @pl.when((z < n - 1) & ((z >= pivot) | (h < ahead)))
         def _():
             gate(h).start()
 
@@ -174,8 +175,11 @@
 
     lane = lax.broadcasted_iota(jnp.int32, (rows, HD), 1) // width
 
-    @pl.loop(0, heads)
-    def _(h):
+    def mix(h):
+        @pl.when((z < pivot) & (h >= ahead))
+        def _():
+            gate(h).start()
+
         @pl.when(z > 0)
         def _():
             gate(h).wait_recv()
@@ -216,7 +220,7 @@
             ll = lst[h, gi, :, at:at + rows]
             aa = ast[h, gi, :, at:at + rows]
             sbuf[s - 1, h] = (aa * (1.0 / ll[0:1])).astype(BF)
-            sstat[s - 1, h] = mm + jnp.log(ll)
+            sstat[s - 1, h] = mm[0:1] + jnp.log(ll[0:1])
             o.start()
             t.start()
         each_part(h, act)
@@ -242,12 +246,14 @@
     def _():
         @pl.loop(0, heads)
         def _(h):
+            mix(h)
             own_keys(h)
             hand_over(h)
 
     def one_head(h):
         @pl.when(z <= pivot)
         def _():
+            mix(h)
             own_keys(h)
 
         @pl.loop(0, jnp.where(z <= pivot, z, 0))
@@ -394,8 +400,8 @@
         vm((pivot + 1, heads, rows, HD), BF), vm((pivot + 1, heads, HD, rows), BF),
         vm((heads, padded * rows, HD), BF),
         vm((heads, gq, 8, span), F32), vm((heads, gq, 8, span), F32), vm((heads, gq, HD, span), F32),
-        vm((parts, heads, HD, rows), BF), vm((parts, heads, 8, rows), F32),
-        vm((parts, heads, HD, rows), BF), vm((parts, heads, 8, rows), F32),
+        vm((parts, heads, HD, rows), BF), vm((parts, heads, 1, rows), F32),
+        vm((parts, heads, HD, rows), BF), vm((parts, heads, 1, rows), F32),
         vm((heads // 2, rows, 2 * HD), BF), vm((channels, total), BF), vm((m, rows, cols), F32),
     ] + [vm((chips, 4, rows, cols // 4), BF)] * 4 + [
         dma, dma((heads,)), dma((heads,)), dma, dma, dma, dma((heads,)), dma((heads,)),

time: 38.2 us -> 37.2 us (0.974)
  Pallas kernels: 37.4 us -> 36.4 us
    pallas_call x1, Pallas kernels: 37.4 us -> 36.4 us  [per_device(): pl.pallas_call(functools.partial(kernel, n, m), out_shape=pltpu.VMEM((row...]
where the time goes in v4:
time: 37.2 us; the launch traced here: 37.1 us
  Pallas kernels  36.4 us (98%)
  local copies, waits for them, and re-layouts  0.71 us (2%)
    pallas_call x1, Pallas kernels, per_device(): pl.pallas_call(functools.partial(kernel, n, m), out_shape=pltpu.VMEM((row...  36.4 us

profile of v4, /device:TPU:28, one launch (start us, length us, event | category | flops | bytes accessed | tf_op | source)
XLA Modules:
  0.0 37.1 jit_solution(11851048321719844823)
XLA Ops:
  0.0 36.4 %shard_map.73 = bf16[128,1024]{1,0:T(8,128)(2,1)S(1)} custom-call(bf16[3,128,1024]{2,1,0:T(8,128)(2,1)} %bitcast.2, bf16[3,3,1024]{2,1,0:T(4,128)(2,1)} %sf_hbm.1, bf16[64,128]{1,0:T(8,128)(2,1)} %lf_hbm.1, f32[1,1024]{1,0:T(1,128)} %bitcast.3, bf16[128,1024]{1,0:T(8,128)(2,1)} %q_hbm.1, bf16[128,1024]{1,0:T(8,128)(2,1)} %k_hbm.1, bf16[1024,4096]{1,0:T(8,128)(2,1)} %w_hbm.1), custom_call_target="tpu_custom_call" | custom-call | tf_op jit(solution)/shard_map/pallas_call | solution.py:413
  36.4 0.7 %copy.9 = bf16[128,1024]{1,0:T(8,128)(2,1)} copy(bf16[128,1024]{1,0:T(8,128)(2,1)S(1)} %shard_map.73) | data formatting | bytes 524288
